TPU v7x, 32 devices: a whole 2x2x4 slice. The times are simulated.
32 devices in a mesh: row: 8 (over y, x, core), col: 4 (over z).
Axes of the slice: x: 2, y: 2, z: 4, core: 2. Of those that a mesh axis runs over, the one named last changes fastest.
Arguments:
- inverse: float32 [20480, 20480], P('row', 'col'), may hold values from -6 to 6
- factor: float32 [20480, 2, 256], P(('row', 'col')), may hold values from -0.0390625 to 0.0390625
- diag_inverse: float32 [2, 256, 256], replicated, may hold values from -6 to 6
- block_sizes: int32 [64], replicated, may hold values from 1 to 1280, 20480 in all
- listed: int32 [2, 64], replicated, may hold values 0 or 1
Outputs:
- ancestor_rows: float32 [20480, 2, 256], P(('row', 'col'))
- diagonal_block: float32 [2, 256, 256], replicated
Inputs may be any that keep to these rules, and one draw needn't show every extreme that they name: `block_sizes`: positive sizes that sum to 20480; the largest is exactly 1280.
All inputs are finite; a program needn't handle non-finite values.
Results may differ from a plain program's by a relative error of at most 0.00007.
Values sent between devices are 32-bit elements; how exact they have to be, the bound alone decides.
A program may use at most 128 MiB of HBM per device.

v0:
```python
import jax
import jax.numpy as jnp
from jax import lax
from jax.sharding import PartitionSpec as P


def from_root(value, axis, source):
    kept = jnp.where(lax.axis_index(axis) == source, value, 0).astype(value.dtype)
    return lax.psum(kept, axis)


def membership(first_row, row_total, block_sizes, listed):
    block_ends = jnp.cumsum(block_sizes)
    block_starts = block_ends - block_sizes
    positions = first_row + jnp.arange(row_total, dtype=jnp.int32)
    inside = (
        (positions[:, None] >= block_starts[None, :]) & (positions[:, None] < block_ends[None, :])
    ).astype(jnp.float32)
    return jnp.dot(
        inside,
        listed.astype(jnp.float32).T,
        precision=lax.Precision.HIGHEST,
        preferred_element_type=jnp.float32,
    )


def per_device(inverse, factor, diag_inverse, block_sizes, listed):
    n_rowdev = lax.axis_size("row")
    n_coldev = lax.axis_size("col")
    row_place = lax.axis_index("row")
    col_place = lax.axis_index("col")
    shard_rows = factor.shape[0]
    sibling_count = factor.shape[1]
    width = factor.shape[2]
    ratio = n_rowdev // n_coldev
    row_block = lax.all_gather(factor, "col", axis=0, tiled=True)
    gathered = []
    for offset in range(ratio):
        gathered.append(from_root(row_block, "row", col_place * ratio + offset))
    col_block = jnp.concatenate(gathered, axis=0)
    col_rows = col_block.shape[0]
    col_member = membership(col_place * col_rows, col_rows, block_sizes, listed)
    panel = (col_block * col_member[:, :, None]).reshape(col_rows, sibling_count * width)
    block_total = inverse.shape[0]
    partial_value = -jnp.dot(
        inverse, panel, precision=lax.Precision.HIGHEST, preferred_element_type=jnp.float32
    )
    summed = lax.psum(partial_value, "col")
    block_member = membership(row_place * block_total, block_total, block_sizes, listed)
    block_result = summed.reshape(block_total, sibling_count, width) * block_member[:, :, None]
    schur_term = jnp.einsum(
        "isw,isv->swv", row_block, block_result, precision=lax.Precision.HIGHEST
    )
    schur = lax.psum(schur_term, "row")
    ancestor_rows = lax.dynamic_slice_in_dim(block_result, col_place * shard_rows, shard_rows, 0)
    return (ancestor_rows, diag_inverse - schur)


def solution(mesh):
    in_specs = (P("row", "col"), P(("row", "col"), None, None), P(), P(), P())
    out_specs = (P(("row", "col"), None, None), P())
    return jax.shard_map(
        per_device, mesh=mesh, in_specs=in_specs, out_specs=out_specs, check_vma=False
    )
```

profile of v0, /device:TPU:0, one launch (start us, length us, event | category | flops | bytes accessed | tf_op | source)
XLA Modules:
  0.0 653.9 jit_solution(9232629267015286627)
XLA Ops:
  7.2 0.0 all-gather.2.cloned.1.call-start
  7.2 2.5 copy.24
  9.7 0.0 all-gather.2.cloned.1.call-update
  9.7 0.0 all-reduce.9.cloned.1.call-start
  9.8 101.1 %all-gather.2.cloned.1.call-done = f32[2560,2,256]{2,0,1:T(8,128)} async-done(((f32[640,2,256]{2,0,1:T(8,128)}), f32[2560,2,256]{2,0,1:T(8,128)}) %all-gather.2.cloned.1.call-update) | async-done | bytes 5242896 | tf_op jit(solution)/shard_map/all_gather | solution.py:36
  110.9 7.2 %broadcast_select_fusion.1 = (f32[2560,2,256]{2,0,1:T(8,128)}, f32[2560,2,256]{2,0,1:T(8,128)}) fusion(f32[2560,2,256]{2,0,1:T(8,128)} %all-gather.2.cloned.1.call-done, pred[]{:T(512)S(6)} %eq.6, pred[]{:T(512)S(6)} %eq.7), kind=kLoop, calls=%fused_computation.9 | loop fusion | flops 2621440 | bytes 15728642 | tf_op jit(solution)/shard_map/jit(_where)/select_n | solution.py:8
  118.1 5.9 copy.25
  124.0 5.9 copy.26
  129.9 0.0 copy-start.3
  129.9 0.0 copy-start.2
  129.9 0.0 all-reduce.9.cloned.1.call-update
  130.0 0.0 all-reduce.5.cloned.1.call-start
  130.0 0.6 copy-done.3
  130.6 0.1 copy.27
  130.7 0.1 reduce-window.8
  130.8 0.1 reduce
  130.9 0.0 copy-done.2
  130.9 0.6 fusion.10
  131.6 146.0 %all-reduce.9.cloned.1.call-done = (f32[2560,512]{0,1:T(8,128)}, f32[2560,512]{0,1:T(8,128)}) async-done(((f32[2560,512]{0,1:T(8,128)}, f32[2560,512]{0,1:T(8,128)}), (f32[2560,512]{0,1:T(8,128)}, f32[2560,512]{0,1:T(8,128)})) %all-reduce.9.cloned.1.call-update) | async-done | bytes 10485776 | tf_op jit(solution)/shard_map/psum | solution.py:9
  277.5 5.2 mul.34
  282.8 91.4 %fusion.5 = f32[512,2560]{1,0:T(8,128)} fusion(f32[2560,5120]{1,0:T(8,128)} %param.5, f32[5120,512]{0,1:T(8,128)} %bitcast.14, f32[2560,512]{0,1:T(8,128)} %get-tuple-element.8, f32[2560,512]{0,1:T(8,128)} %get-tuple-element.9), kind=kOutput, calls=%fused_computation.6 | convolution fusion | flops 80537190400 | bytes 78643200 | tf_op jit(solution)/shard_map/dot_general | solution.py:45
  374.2 8.7 %copy.28 = f32[2560,2,256]{2,1,0:T(2,128)} copy(f32[2560,2,256]{0,2,1:T(8,128)} %bitcast.15) | data formatting | bytes 10485760 | tf_op jit(solution)/shard_map/reshape | solution.py:50
  382.9 0.0 all-reduce.5.cloned.1.call-update
  382.9 0.2 all-reduce.7.cloned.1.call-start
  383.2 0.9 fusion.6
  384.0 188.0 %all-reduce.5.cloned.1.call-done = f32[2560,2,256]{2,1,0:T(2,128)} async-done(((f32[2560,2,256]{2,1,0:T(2,128)}), f32[2560,2,256]{2,1,0:T(2,128)}) %all-reduce.5.cloned.1.call-update) | async-done | bytes 5242896 | tf_op jit(solution)/shard_map/psum | solution.py:48
  572.1 5.5 broadcast_multiply_fusion
  577.6 0.0 copy-start
  577.6 2.3 copy-done
  579.9 0.0 copy-start.1
  579.9 11.5 %fusion.11 = f32[2,256,256]{1,2,0:T(8,128)} fusion(f32[2560,2,256]{2,0,1:T(8,128)} %all-gather.2.cloned.1.call-done, f32[2560,2,256]{2,1,0:T(2,128)S(1)} %broadcast_multiply_fusion), kind=kOutput, calls=%fused_computation.16 | convolution fusion | flops 4026531840 | bytes 11010048 | tf_op jit(solution)/shard_map/isw,isv->swv/dot_general | solution.py:51
  591.4 0.0 all-reduce.7.cloned.1.call-update
  591.4 0.0 copy-done.1
  591.4 0.2 copy.31
  591.6 2.8 constant_dynamic-slice_fusion
  594.4 50.8 %all-reduce.7.cloned.1.call-done = f32[2,256,256]{1,2,0:T(8,128)} async-done(((f32[2,256,256]{1,2,0:T(8,128)}), f32[2,256,256]{1,2,0:T(8,128)}) %all-reduce.7.cloned.1.call-update) | async-done | bytes 524304 | tf_op jit(solution)/shard_map/psum | solution.py:54
  645.3 1.1 sub.8
  646.4 1.0 copy.32
  (3 shorter events, 0.0 us)
Async XLA Ops:
  7.2 103.7 %all-gather.2.cloned.1.call-start = ((), (), s32[]{:S(2)}) async-start(), calls=%async_computation | async-start | bytes 6553600 | tf_op jit(solution)/shard_map/all_gather | solution.py:36
  9.7 267.8 %all-reduce.9.cloned.1.call-start = ((), (), s32[]{:S(2)}) async-start(), calls=%async_computation.3 | async-start | bytes 20971520 | tf_op jit(solution)/shard_map/psum | solution.py:9
  129.9 0.7 copy-start.3
  129.9 1.0 copy-start.2
  130.0 442.1 %all-reduce.5.cloned.1.call-start = ((), (), s32[]{:S(2)}) async-start(), calls=%async_computation.1 | async-start | bytes 10485760 | tf_op jit(solution)/shard_map/psum | solution.py:48
  382.9 262.4 %all-reduce.7.cloned.1.call-start = ((), (), s32[]{:S(2)}) async-start(), calls=%async_computation.2 | async-start | bytes 1048576 | tf_op jit(solution)/shard_map/psum | solution.py:54
  577.6 2.3 copy-start
  579.9 11.5 %copy-start.1 = (f32[2,256,256]{2,1,0:T(8,128)S(1)}, f32[2,256,256]{2,1,0:T(8,128)}, u32[]{:S(2)}) copy-start(f32[2,256,256]{2,1,0:T(8,128)} %param.7) | copy-start | bytes 1572868
Sparse Core Ops, SparseCore 0:
  10.1 100.7 all-gather.1
  130.1 147.3 all-reduce.8
  383.0 188.9 all-reduce.4
  591.5 53.7 all-reduce.6
where the time goes:
time: 655 us; the launch traced here: 654 us
  waiting for transfers between devices  486 us (74%)
  matrix products  104 us (16%)
  local copies, waits for them, and re-layouts  35.2 us (5%)
  other arithmetic  14.1 us (2%)
  between operations  13.9 us (2%)
    psum x1, waiting for transfers between devices, per_device(): summed = lax.psum(partial_value, 'col')  188 us
    psum x1, waiting for transfers between devices, from_root(): return lax.psum(kept, axis)  146 us
    all_gather x1, waiting for transfers between devices, per_device(): row_block = lax.all_gather(factor, 'col', axis=0, tiled=True)  101 us
    dot_general x1, matrix products, per_device(): jnp.dot(inverse, panel, precision=lax.Precision.HIGHEST, preferred_elemen...  91.4 us
    psum x1, waiting for transfers between devices, per_device(): schur = lax.psum(schur_term, 'row')  50.8 us
  transfers between devices with their start and end apart: 4, of which 4 were waited for; matrix products, arithmetic and copies ran while one was open for 1% of the time, Pallas kernels for 0%

commit v1 on v0

--- a/solution.py
+++ b/solution.py
@@ -45,7 +45,10 @@
     partial_value = -jnp.dot(
         inverse, panel, precision=lax.Precision.HIGHEST, preferred_element_type=jnp.float32
     )
-    summed = lax.psum(partial_value, "col")
+    size, summed = (lax.axis_size("col"), partial_value)
+    for far in [1 << k for k in range(size.bit_length() - 1)]:
+        route = [(i, i ^ far) for i in range(size)]
+        summed = summed + lax.ppermute(summed, "col", route)
     block_member = membership(row_place * block_total, block_total, block_sizes, listed)
     block_result = summed.reshape(block_total, sibling_count, width) * block_member[:, :, None]
     schur_term = jnp.einsum(

time: 655 us -> 820 us (1.25)
  waiting for transfers between devices: 486 us -> 637 us
  other arithmetic: 14.1 us -> 27.4 us
    ppermute x0 -> x2, waiting for transfers between devices: none -> 337 us  [per_device(): summed = summed + lax.ppermute(summed, 'col', route)]
    psum x1 -> x0, waiting for transfers between devices: 188 us -> none  [per_device(): summed = lax.psum(partial_value, 'col')]
    add x0 -> x2, other arithmetic: none -> 13.2 us  [per_device(): summed = summed + lax.ppermute(summed, 'col', route)]
  transfers between devices with their start and end apart: 4 -> 5, of which waited for: 4 -> 5; matrix products, arithmetic and copies ran while one was open for 1% -> 1% of each run, Pallas kernels for 0% -> 0%
where the time goes in v1:
time: 820 us; the launch traced here: 819 us
  waiting for transfers between devices  637 us (78%)
  matrix products  102 us (12%)
  local copies, waits for them, and re-layouts  35.4 us (4%)
  other arithmetic  27.4 us (3%)
  between operations  13.9 us (2%)
    ppermute x2, waiting for transfers between devices, per_device(): summed = summed + lax.ppermute(summed, 'col', route)  337 us
    psum x1, waiting for transfers between devices, from_root(): return lax.psum(kept, axis)  146 us
    all_gather x1, waiting for transfers between devices, per_device(): row_block = lax.all_gather(factor, 'col', axis=0, tiled=True)  101 us
    dot_general x1, matrix products, per_device(): jnp.dot(inverse, panel, precision=lax.Precision.HIGHEST, preferred_elemen...  91.4 us
    psum x1, waiting for transfers between devices, per_device(): schur = lax.psum(schur_term, 'row')  52.3 us
  transfers between devices with their start and end apart: 5, of which 5 were waited for; matrix products, arithmetic and copies ran while one was open for 1% of the time, Pallas kernels for 0%

profile of v1, /device:TPU:0, one launch (start us, length us, event | category | flops | bytes accessed | tf_op | source)
XLA Modules:
  0.0 819.5 jit_solution(10184631163930240483)
XLA Ops:
  7.2 0.0 all-gather.2.cloned.1.call-start
  7.2 2.5 copy.24
  9.7 0.0 all-gather.2.cloned.1.call-update
  9.7 0.0 all-reduce.6.cloned.1.call-start
  9.8 101.1 %all-gather.2.cloned.1.call-done = f32[2560,2,256]{2,0,1:T(8,128)} async-done(((f32[640,2,256]{2,0,1:T(8,128)}), f32[2560,2,256]{2,0,1:T(8,128)}) %all-gather.2.cloned.1.call-update) | async-done | bytes 5242896 | tf_op jit(solution)/shard_map/all_gather | solution.py:36
  110.9 7.2 broadcast_select_fusion.1
  118.1 5.9 copy.25
  124.0 5.9 copy.26
  130.0 0.0 copy-start.3
  130.0 0.0 copy-start.2
  130.0 0.0 all-reduce.6.cloned.1.call-update
  130.0 0.0 all-reduce.4.cloned.1.call-start
  130.1 0.6 copy-done.3
  130.6 0.1 copy.27
  130.7 0.1 reduce-window.8
  130.8 0.1 reduce
  131.0 0.0 copy-done.2
  131.0 0.6 fusion.9
  131.6 146.0 %all-reduce.6.cloned.1.call-done = (f32[2560,512]{0,1:T(8,128)}, f32[2560,512]{0,1:T(8,128)}) async-done(((f32[2560,512]{0,1:T(8,128)}, f32[2560,512]{0,1:T(8,128)}), (f32[2560,512]{0,1:T(8,128)}, f32[2560,512]{0,1:T(8,128)})) %all-reduce.6.cloned.1.call-update) | async-done | bytes 10485776 | tf_op jit(solution)/shard_map/psum | solution.py:9
  277.6 5.2 mul.34
  282.8 91.4 %negate_bitcast_fusion = f32[2560,512]{0,1:T(8,128)} fusion(f32[2560,5120]{1,0:T(8,128)} %param.5, f32[5120,512]{0,1:T(8,128)} %bitcast.18, f32[2560,512]{0,1:T(8,128)} %get-tuple-element.8, f32[2560,512]{0,1:T(8,128)} %get-tuple-element.9), kind=kOutput, calls=%fused_computation.6 | convolution fusion | flops 80537190400 | bytes 78643200 | tf_op jit(solution)/shard_map/dot_general | solution.py:45
  374.2 1.5 collective-permute-start
  375.7 113.2 %collective-permute-done = f32[2560,512]{0,1:T(8,128)S(1)} collective-permute-done((f32[2560,512]{0,1:T(8,128)}, f32[2560,512]{0,1:T(8,128)S(1)}, u32[]{:S(2)}, u32[]{:S(2)}) %collective-permute-start) | collective-permute-done | bytes 5242912 | tf_op jit(solution)/shard_map/ppermute | solution.py:51
  488.9 5.8 add.41
  494.8 2.4 collective-permute-start.1
  497.2 0.9 fusion.5
  498.0 223.9 %collective-permute-done.1 = f32[2560,512]{0,1:T(8,128)} collective-permute-done((f32[2560,512]{0,1:T(8,128)}, f32[2560,512]{0,1:T(8,128)}, u32[]{:S(2)}, u32[]{:S(2)}) %collective-permute-start.1) | collective-permute-done | bytes 5242912 | tf_op jit(solution)/shard_map/ppermute | solution.py:51
  722.0 7.4 add.42
  729.4 0.0 slice-start
  729.4 8.8 %copy.29 = f32[2560,2,256]{2,1,0:T(2,128)} copy(f32[2560,2,256]{0,2,1:T(8,128)} %bitcast.17) | data formatting | bytes 10485760 | tf_op jit(solution)/shard_map/reshape | solution.py:53
  738.2 0.0 slice-start.1
  738.2 5.7 broadcast_multiply_fusion
  743.9 0.0 copy-start
  743.9 2.3 copy-done
  746.2 0.0 slice-done
  746.2 0.0 slice-done.1
  746.2 0.0 copy-start.1
  746.2 9.2 %fusion.10 = f32[2,256,256]{1,2,0:T(8,128)} fusion(f32[2560,2,256]{2,0,1:T(8,128)S(1)} %bitcast.14, f32[2560,2,256]{2,1,0:T(2,128)S(1)} %broadcast_multiply_fusion), kind=kOutput, calls=%fused_computation.16 | convolution fusion | flops 4026531840 | bytes 11010048 | tf_op jit(solution)/shard_map/isw,isv->swv/dot_general | solution.py:54
  755.4 0.0 all-reduce.4.cloned.1.call-update
  755.5 0.0 copy-done.1
  755.5 0.2 copy.31
  755.7 2.8 constant_dynamic-slice_fusion
  758.5 52.3 %all-reduce.4.cloned.1.call-done = f32[2,256,256]{1,2,0:T(8,128)} async-done(((f32[2,256,256]{1,2,0:T(8,128)}), f32[2,256,256]{1,2,0:T(8,128)}) %all-reduce.4.cloned.1.call-update) | async-done | bytes 524304 | tf_op jit(solution)/shard_map/psum | solution.py:57
  810.8 1.1 sub.8
  812.0 1.0 copy.32
  (4 shorter events, 0.0 us)
Async XLA Ops:
  7.2 103.7 %all-gather.2.cloned.1.call-start = ((), (), s32[]{:S(2)}) async-start(), calls=%async_computation | async-start | bytes 6553600 | tf_op jit(solution)/shard_map/all_gather | solution.py:36
  9.7 267.9 %all-reduce.6.cloned.1.call-start = ((), (), s32[]{:S(2)}) async-start(), calls=%async_computation.2 | async-start | bytes 20971520 | tf_op jit(solution)/shard_map/psum | solution.py:9
  130.0 0.7 copy-start.3
  130.0 1.0 copy-start.2
  130.0 680.8 %all-reduce.4.cloned.1.call-start = ((), (), s32[]{:S(2)}) async-start(), calls=%async_computation.1 | async-start | bytes 1048576 | tf_op jit(solution)/shard_map/psum | solution.py:57
  374.2 114.7 %collective-permute-start = (f32[2560,512]{0,1:T(8,128)}, f32[2560,512]{0,1:T(8,128)S(1)}, u32[]{:S(2)}, u32[]{:S(2)}) collective-permute-start(f32[2560,512]{0,1:T(8,128)} %negate_bitcast_fusion), channel_id=1, source_target_pairs={{0,1},{1,0},{2,3},{3,2},{4,5},{5,4},{6,7},{7,6},{8,9},{9,8},{10,11... | collective-permute-start | bytes 15728648 | tf_op jit(solution)/shard_map/ppermute | solution.py:51
  494.8 227.2 %collective-permute-start.1 = (f32[2560,512]{0,1:T(8,128)}, f32[2560,512]{0,1:T(8,128)}, u32[]{:S(2)}, u32[]{:S(2)}) collective-permute-start(f32[2560,512]{0,1:T(8,128)} %add.41), channel_id=1, source_target_pairs={{0,2},{1,3},{2,0},{3,1},{4,6},{5,7},{6,4},{7,5},{8,10},{9,11},{10,... | collective-permute-start | bytes 15728648 | tf_op jit(solution)/shard_map/ppermute | solution.py:51
  729.4 16.8 %slice-start = ((s8[5242880]{0:T(1024)(128)(4,1)}), s8[1048576]{0:T(1024)(128)(4,1)S(1)}, s32[]{:S(2)}) async-start(s8[5242880]{0:T(1024)(128)(4,1)} %bitcast.13), calls=%async_computation.3 | async-start | bytes 2097152
  738.2 8.0 slice-start.1
  743.9 2.3 copy-start
  746.2 9.3 %copy-start.1 = (f32[2,256,256]{2,1,0:T(8,128)S(1)}, f32[2,256,256]{2,1,0:T(8,128)}, u32[]{:S(2)}) copy-start(f32[2,256,256]{2,1,0:T(8,128)} %param.7) | copy-start | bytes 1572868
Sparse Core Ops, SparseCore 0:
  10.1 100.7 all-gather.1
  130.1 147.3 all-reduce.5
  755.6 55.2 all-reduce.3
